TPU v7x, 256 devices: a whole 4x4x8 slice. The times are simulated.
256 devices in a mesh: gx: 32 (over z, x), yz: 8 (over y, core).
Axes of the slice: x: 4, y: 4, z: 8, core: 2. Of those that a mesh axis runs over, the one named last changes fastest.
Arguments:
- tensor_slabs: bfloat16 [2048, 32, 1024], P('gx', 'yz'), may hold values from -6 to 6
- slab_counts: int32 [8], replicated, may hold values from 1 to 4, 16 in all
- column_scale: float32 [16, 1024], replicated, may hold values from -6 to 6
- samples: int32 [16, 256], replicated, may hold values from 0 to 1023
Outputs:
- basis_factor: float32 [2048, 256], P('gx')
- core_tensor: bfloat16 [256, 32, 1024], P(None, 'yz', 'gx')
Inputs may be any that keep to these rules, and one draw needn't show every extreme that they name: `slab_counts`: the counts sum to 16; the largest is exactly 4. Slots at or beyond an index's count hold no slab and are not read.
All inputs are finite; a program needn't handle non-finite values.
Results may differ from a plain program's by a relative error of at most 0.0057.
Values may be sent and summed in bfloat16 or wider, within the bound.
No kernel may reach another device: no remote copies, remote signals or barrier semaphores. Data moves between devices by JAX's collectives and lax.ppermute only.
A program may use at most 64 MiB of HBM per device.

v0:
```python
import jax
import jax.numpy as jnp
from jax import lax
from jax.experimental import pallas as pl
from jax.experimental.pallas import tpu as pltpu
from jax.sharding import PartitionSpec as P


F32, BF16, I32 = jnp.float32, jnp.bfloat16, jnp.int32
NN, NT, TN = ((1,), (0,)), ((1,), (1,)), ((0,), (0,))
HIGHEST = lax.Precision.HIGHEST
AHEAD = 9
BLOCK = 64
STEPS = (0, 2, 1, 3)
EARLY = (0, 3)
SLOTS = 4
SHARES = 4
ROOM = pltpu.CompilerParams(vmem_limit_bytes=24 << 20)


def dot(a, b, dims, precision=None):
    return lax.dot_general(
        a, b, (dims, ((), ())), precision=precision, preferred_element_type=F32
    )


def signs(rows, picked):
    both = lax.broadcasted_iota(I32, (rows, picked.shape[1]), 0) & picked
    both = both ^ (both >> 4)
    both = both ^ (both >> 2)
    both = both ^ (both >> 1)
    return (1 - 2 * (both & 1)).astype(F32)


def own_slabs(counts_ref, index, groups):
    offset = jnp.int32(0)
    for group in range(groups):
        offset = offset + jnp.where(group < index, counts_ref[group], 0)
    return offset, counts_ref[index]


def lines_by_slot(tensor_ref):
    rows, slots, width = tensor_ref.shape
    lines = tensor_ref[...].astype(F32).reshape(rows * slots, width).astype(BF16)
    at = lax.broadcasted_iota(I32, (rows * slots, rows * slots), 0)
    of = lax.broadcasted_iota(I32, (rows * slots, rows * slots), 1)
    pick = ((at % rows) * slots + at // rows == of).astype(F32).astype(BF16)
    return dot(pick, lines, NN)


def sketch_kernel(tensor_ref, counts_ref, scale_ref, samples_ref, total_ref, hadamard_ref):
    rows, slots, width = tensor_ref.shape
    total_slabs, sketch = samples_ref.shape
    index = lax.axis_index("yz")
    offset, count = own_slabs(counts_ref, index, counts_ref.shape[0])
    by_slot = lines_by_slot(tensor_ref)
    total = jnp.zeros((rows, sketch), F32)
    for slot in range(slots):
        slab = jnp.minimum(offset + slot, total_slabs - 1)
        picked = samples_ref[pl.ds(slab, 1), :]
        low = signs(32, picked & 31)
        high = signs(width // 32, picked >> 5)
        for part in range(width // 32):
            hadamard_ref[slot, pl.ds(part * 32, 32), :] = (low * high[part : part + 1, :]).astype(BF16)
        piece = by_slot[slot * rows : (slot + 1) * rows]
        scaled = (piece * scale_ref[pl.ds(slab, 1), :]).astype(BF16)
        term = dot(scaled, hadamard_ref[slot], NN)
        total = total + jnp.where(slot < count, term, 0.0)
    total_ref[...] = total * (1.0 / (total_slabs * width) ** 0.5)


def spread_kernel(tensor_ref, moved_ref):
    rows, slots, width = tensor_ref.shape
    by_slot = lines_by_slot(tensor_ref)
    chunk = 128 // slots
    for chunk_index in range(width // chunk):
        start = chunk_index * chunk
        moved_ref[chunk_index] = jnp.concatenate(
            [by_slot[s * rows : (s + 1) * rows, start : start + chunk] for s in range(slots)], axis=1
        ).astype(BF16)


def sketch_part(tensor, counts, scale, samples):
    rows, slots, width = tensor.shape
    sketch = samples.shape[1]
    vmem = pl.BlockSpec(memory_space=pltpu.VMEM)
    return pl.pallas_call(
        sketch_kernel,
        out_shape=pltpu.VMEM((rows, sketch), F32),
        in_specs=[vmem, pl.BlockSpec(memory_space=pltpu.SMEM), vmem, vmem],
        out_specs=vmem,
        scratch_shapes=[pltpu.VMEM((slots, width, sketch), BF16)],
        name="sketch",
    )(tensor, counts, scale, samples)


def spread_columns(tensor):
    rows, slots, width = tensor.shape
    share = width // SHARES
    chunks = share * slots // 128
    return pl.pallas_call(
        spread_kernel,
        out_shape=jax.ShapeDtypeStruct((chunks * SHARES, rows, 128), BF16),
        grid=(SHARES,),
        in_specs=[pl.BlockSpec((rows, slots, share), lambda number: (0, 0, number))],
        out_specs=pl.BlockSpec((chunks, rows, 128), lambda number: (number, 0, 0)),
        name="spread",
    )(tensor)


def block_inverse(tiles, first):
    count = len(tiles)
    size = 8 * count
    lines = list(tiles)
    sub = lax.broadcasted_iota(I32, (8, 128), 0)
    lane = lax.broadcasted_iota(I32, (8, 128), 1) - first

    def row_of(tile, at):
        return jnp.broadcast_to(tile[at : at + 1, :], (8, 128))

    def column_of(tile, at):
        return jnp.broadcast_to(tile[:, first + at : first + at + 1], (8, 128))

    columns = {j: [column_of(tile, j) for tile in lines] for j in range(min(AHEAD, size))}
    pivots = [jnp.ones((8, 128), F32)] * count
    for step in range(size):
        tile, at = divmod(step, 8)
        column = columns.pop(step)
        pivot = row_of(column[tile], at)
        pivots[tile] = jnp.where(sub == at, pivot, pivots[tile])
        if step == size - 1:
            break
        inverse = 1.0 / pivot
        factors = {t: column[t] * inverse for t in range(tile, count)}
        factors[tile] = jnp.where(sub > at, factors[tile], 0.0)
        if at == 7:
            factors.pop(tile)
        for later in columns.values():
            value = row_of(later[tile], at)
            for t, factor in factors.items():
                later[t] = later[t] - factor * value
        line = jnp.where(lane == step, 1.0, row_of(lines[tile], at))
        for t, factor in factors.items():
            cleared = (lane == step) if t > tile else (lane == step) & (sub > at)
            lines[t] = jnp.where(cleared, 0.0, lines[t]) - factor * line
        new = step + AHEAD
        if new < size:
            columns[new] = [column_of(lines[t], new) if t >= (step + 1) // 8 else None for t in range(count)]
    result = []
    for t in range(count):
        inside = jnp.where(lane == sub + 8 * t, 1.0, 0.0)
        inside = jnp.where((lane >= 0) & (lane < sub + 8 * t), lines[t], inside)
        result.append(lax.rsqrt(pivots[t]) * inside)
    return jnp.concatenate(result, 0)


def invert_factor(work_ref):
    size = work_ref.shape[0]
    lanes = lax.broadcasted_iota(I32, (1, size), 1)
    block = work_ref[0:BLOCK, 0:128]
    for start in range(0, size, BLOCK):
        end = start + BLOCK
        after = end + BLOCK
        group = start // 128 * 128
        first = start - group
        inverse = block_inverse([block[8 * t : 8 * t + 8] for t in range(BLOCK // 8)], first)
        here = (lanes >= start) & (lanes < end)
        placed = [jnp.zeros((BLOCK, 128), F32)] * (size // 128)
        placed[group // 128] = inverse
        line = jnp.where(here, jnp.concatenate(placed, 1), dot(inverse, work_ref[group : group + 128, :], NN, HIGHEST))
        if end < size:
            below = dot(work_ref[end:after, group : group + 128], inverse, NT, HIGHEST)
            new = jnp.where(here, 0.0, work_ref[end:after, :]) - dot(below, line, NN, HIGHEST)
            block = new[:, end // 128 * 128 : end // 128 * 128 + 128]
        if after < size:
            rest = dot(work_ref[after:, group : group + 128], inverse, NT, HIGHEST)
            work_ref[after:, :] = jnp.where(here, 0.0, work_ref[after:, :]) - dot(rest, line, NN, HIGHEST)
        work_ref[start:end, :] = line
        if end < size:
            work_ref[end:after, :] = new
    row = lax.broadcasted_iota(I32, (size, size), 0)
    column = lax.broadcasted_iota(I32, (size, size), 1)
    work_ref[...] = jnp.where(row >= column, work_ref[...], 0.0)


def halves(array):
    high = array.astype(BF16)
    return high, (array - high.astype(F32)).astype(BF16)


def gram_of(pieces):
    square = cross = None
    for piece in pieces:
        flat = piece[...].reshape(-1, piece.shape[-1])
        high, rest = halves(flat)
        low = (flat - high.astype(F32) - rest.astype(F32)).astype(BF16)
        even = dot(high, high, TN) + dot(rest, rest, TN)
        odd = dot(high, rest, TN) + dot(high, low, TN)
        square = even if square is None else square + even
        cross = odd if cross is None else cross + odd
    return square + (cross + cross.T)


def gram_kernel(*refs):
    refs[-1][...] = gram_of(refs[:-1])


def factor_kernel(*refs):
    pieces, gram_ref, inverse_ref = refs[:-2], refs[-2], refs[-1]
    inverse_ref[...] = gram_ref[...] + gram_of(pieces)
    invert_factor(inverse_ref)


def core_kernel(*refs):
    pieces, (inverse_ref, moved_ref, counts_ref, basis_ref, core_ref), scratch = refs[:8], refs[8:13], refs[13:]
    rows_ref, block_ref = scratch
    blocks, parts, line, size = rows_ref.shape
    index = lax.axis_index("yz")
    core, chip = index % 2, index // 2
    chips = parts // 2
    inverse = inverse_ref[...]
    inverse_high, inverse_low = halves(inverse)
    for number, piece in enumerate(pieces):
        which, step = divmod(number, chips)
        place = 2 * ((chip + chips - STEPS[step]) % chips) + (core if which == 0 else 1 - core)
        block_ref[place] = piece[lax.axis_index("gx")]
        high, low = halves(piece[...].reshape(blocks * line, size))
        rows = dot(high, inverse_high, NT) + dot(high, inverse_low, NT) + dot(low, inverse_high, NT)
        rows_ref[:, place] = rows.reshape(blocks, line, size)
    basis_ref[...] = dot(block_ref[...].reshape(parts * line, size), inverse, NT, HIGHEST)
    every = rows_ref[...].reshape(blocks * parts * line, size).astype(BF16)
    result = dot(moved_ref[...].reshape(blocks * parts * line, 128), every, TN)
    slot = lax.broadcasted_iota(I32, result.shape, 0) // (128 // SLOTS)
    core_ref[...] = jnp.where(slot < counts_ref[index], result, 0.0).astype(BF16)


def near(*arrays):
    return tuple(pltpu.with_memory_space_constraint(each, pltpu.VMEM) for each in arrays)


def gram_part(*pieces):
    size = pieces[0].shape[-1]
    vmem = pl.BlockSpec(memory_space=pltpu.VMEM)
    return pl.pallas_call(
        gram_kernel,
        out_shape=pltpu.VMEM((size, size), F32),
        in_specs=[vmem] * len(pieces),
        out_specs=vmem,
        name="gram",
        compiler_params=ROOM,
    )(*near(*pieces))


def inverse_factor(pieces, gram):
    size = gram.shape[0]
    vmem = pl.BlockSpec(memory_space=pltpu.VMEM)
    return pl.pallas_call(
        factor_kernel,
        out_shape=pltpu.VMEM((size, size), F32),
        in_specs=[vmem] * (len(pieces) + 1),
        out_specs=vmem,
        name="factor",
        compiler_params=ROOM,
    )(*near(*pieces, gram))


def core_and_basis(pieces, inverse, moved, counts):
    blocks, line, size = pieces[0].shape
    parts = len(pieces)
    vmem = pl.BlockSpec(memory_space=pltpu.VMEM)
    return pl.pallas_call(
        core_kernel,
        out_shape=(
            jax.ShapeDtypeStruct((parts * line, size), F32),
            jax.ShapeDtypeStruct((128, size), BF16),
        ),
        in_specs=[vmem] * (parts + 2) + [pl.BlockSpec(memory_space=pltpu.SMEM)],
        out_specs=(vmem, vmem),
        scratch_shapes=[
            pltpu.VMEM((blocks, parts, line, size), F32),
            pltpu.VMEM((parts, line, size), F32),
        ],
        name="core",
        compiler_params=ROOM,
    )(*near(*pieces, inverse, moved), counts)


def local(tensor_slabs, slab_counts, column_scale, samples):
    _, slots, _ = tensor_slabs.shape
    sketch = samples.shape[1]
    blocks = lax.axis_size("gx")
    members = lax.axis_size("yz")
    swap = [(j, j ^ 1) for j in range(members)]
    total = sketch_part(tensor_slabs, slab_counts, column_scale, samples)
    parts = lax.all_to_all(total.reshape(members, -1, sketch), "yz", 0, 0, tiled=True)
    part = jnp.broadcast_to(parts.sum(0), (blocks, *parts.shape[1:]))
    column = lax.all_to_all(part, "gx", 0, 0, tiled=True)
    pieces = [column]
    for step in STEPS[1:]:
        turn = [(j, (j + 2 * step) % members) for j in range(members)]
        pieces.append(lax.ppermute(column, "yz", turn))
    chunks = spread_columns(tensor_slabs)
    moved = lax.all_to_all(chunks, "gx", 0, 0, tiled=True)
    live = jnp.minimum(slab_counts, slots)
    pieces = pieces + [lax.ppermute(piece, "yz", swap) for piece in pieces]
    gram = gram_part(*(piece for number, piece in enumerate(pieces) if number % len(STEPS) in EARLY))
    rest = [piece for number, piece in enumerate(pieces) if number % len(STEPS) not in EARLY]
    inverse = inverse_factor(rest, gram)
    basis, core = core_and_basis(pieces, inverse, moved, live)
    core = jnp.moveaxis(core.reshape(slots, -1, sketch), 2, 0)
    return basis, core


def solution(mesh):
    placed = (P("gx", "yz", None), P(), P(), P())
    return jax.shard_map(
        local,
        mesh=mesh,
        in_specs=placed,
        out_specs=(P("gx", None), P(None, "yz", "gx")),
        check_vma=False,
    )
```

profile of v0, /device:TPU:1, one launch (start us, length us, event | category | flops | bytes accessed | tf_op | source)
XLA Modules:
  0.0 70.2 jit_solution(14631603266837138236)
XLA Ops:
  0.6 1.9 %sketch.1 = f32[64,256]{1,0:T(8,128)S(1)} custom-call(bf16[64,4,1024]{2,1,0:T(4,128)(2,1)} %tensor_ref.3, s32[8]{0:T(128)} %counts_ref.1, f32[16,1024]{1,0:T(8,128)} %scale_ref.1, s32[16,256]{1,0:T(8,128)} %samples_ref.1), custom_call_target="tpu_custom_call" | custom-call | tf_op jit(solution)/shard_map/sketch/pallas_call | solution.py:87
  2.5 10.6 %all_to_all.15 = f32[8,8,256]{2,1,0:T(8,128)S(1)} all-to-all(f32[8,8,256]{2,1,0:T(8,128)S(1)} %bitcast.4), channel_id=1, replica_groups=mesh['gx'=32,'yz'=8] {'yz'}, dimensions={0} | all-to-all | bytes 131072 | tf_op jit(solution)/shard_map/all_to_all | solution.py:295
  13.1 0.7 %broadcast_in_dim.3 = f32[32,8,256]{2,1,0:T(8,128)} broadcast(f32[8,256]{1,0:T(8,128)S(1)} %reduce_sum.9), dimensions={1,2} | broadcast | bytes 270336 | tf_op jit(solution)/shard_map/broadcast_in_dim | solution.py:296
  13.8 11.0 %all-to-all-start.1 = ((f32[32,8,256]{2,1,0:T(8,128)}), f32[32,8,256]{2,1,0:T(8,128)S(1)}, u32[]{:S(2)}, u32[]{:S(2)}) async-start(f32[32,8,256]{2,1,0:T(8,128)} %broadcast_in_dim.3), calls=%async_computation.1 | async-start | bytes 524288 | tf_op jit(solution)/shard_map/all_to_all | solution.py:297
  24.9 3.8 %spread.1 = bf16[32,64,128]{2,1,0:T(8,128)(2,1)} custom-call(bf16[64,4,1024]{2,1,0:T(4,128)(2,1)} %tensor_ref.3), custom_call_target="tpu_custom_call" | custom-call | tf_op jit(solution)/shard_map/spread/pallas_call | solution.py:101
  28.7 0.0 copy-start
  28.7 7.5 %all-to-all-done.1.refs_0_ = f32[32,8,256]{2,1,0:T(8,128)S(1)} async-done(((f32[32,8,256]{2,1,0:T(8,128)}), f32[32,8,256]{2,1,0:T(8,128)S(1)}, u32[]{:S(2)}, u32[]{:S(2)}) %all-to-all-start.1) | async-done | bytes 262176 | tf_op jit(solution)/shard_map/all_to_all | solution.py:297
  36.2 4.7 %all-to-all-start.2 = ((bf16[32,64,128]{2,1,0:T(8,128)(2,1)}), bf16[32,64,128]{2,1,0:T(8,128)(2,1)S(1)}, u32[]{:S(2)}, u32[]{:S(2)}) async-start(bf16[32,64,128]{2,1,0:T(8,128)(2,1)} %spread.1), calls=%async_computation.2 | async-start | bytes 1048576 | tf_op jit(solution)/shard_map/all_to_all | solution.py:303
  40.9 1.0 %collective-permute-start.2 = (f32[32,8,256]{2,1,0:T(8,128)S(1)}, f32[32,8,256]{2,1,0:T(8,128)S(1)}, u32[]{:S(2)}, u32[]{:S(2)}) collective-permute-start(f32[32,8,256]{2,1,0:T(8,128)S(1)} %all-to-all-done.1.refs_0_), channel_id=1, source_target_pairs={{0,6},{1,7},{2,0},{3,1},{4,2},{5,3},{6,4},{7,5},{8,14},{9,15},{10,... | collective-permute-start | bytes 786440 | tf_op jit(solution)/shard_map/ppermute | solution.py:301
  41.9 1.2 %collective-permute-start = (f32[32,8,256]{2,1,0:T(8,128)S(1)}, f32[32,8,256]{2,1,0:T(8,128)S(1)}, u32[]{:S(2)}, u32[]{:S(2)}) collective-permute-start(f32[32,8,256]{2,1,0:T(8,128)S(1)} %all-to-all-done.1.refs_0_), channel_id=1, source_target_pairs={{0,4},{1,5},{2,6},{3,7},{4,0},{5,1},{6,2},{7,3},{8,12},{9,13},{10,... | collective-permute-start | bytes 786440 | tf_op jit(solution)/shard_map/ppermute | solution.py:301
  43.0 0.0 collective-permute-start.1
  43.1 2.3 %collective-permute-start.3 = (f32[32,8,256]{2,1,0:T(8,128)S(1)}, f32[32,8,256]{2,1,0:T(8,128)S(1)}, u32[]{:S(2)}, u32[]{:S(2)}) collective-permute-start(f32[32,8,256]{2,1,0:T(8,128)S(1)} %all-to-all-done.1.refs_0_), channel_id=1, source_target_pairs={{0,1},{1,0},{2,3},{3,2},{4,5},{5,4},{6,7},{7,6},{8,9},{9,8},{10,11... | collective-permute-start | bytes 786440 | tf_op jit(solution)/shard_map/ppermute | solution.py:305
  45.3 1.8 %collective-permute-done.2.refs_1_.refs_3_ = f32[32,8,256]{2,1,0:T(8,128)S(1)} collective-permute-done((f32[32,8,256]{2,1,0:T(8,128)S(1)}, f32[32,8,256]{2,1,0:T(8,128)S(1)}, u32[]{:S(2)}, u32[]{:S(2)}) %collective-permute-start.2) | collective-permute-done | bytes 262176 | tf_op jit(solution)/shard_map/ppermute | solution.py:301
  47.1 4.8 %collective-permute-start.6 = (f32[32,8,256]{2,1,0:T(8,128)S(1)}, f32[32,8,256]{2,1,0:T(8,128)S(1)}, u32[]{:S(2)}, u32[]{:S(2)}) collective-permute-start(f32[32,8,256]{2,1,0:T(8,128)S(1)} %collective-permute-done.2.refs_1_.refs_3_), channel_id=1, source_target_pairs={{0,1},{1,0},{2,3},{3,2},{4,5},{5,4},{6,7},{7,6},{8,9},{9,8},{10,11... | collective-permute-start | bytes 786440 | tf_op jit(solution)/shard_map/ppermute | solution.py:305
  51.9 0.0 collective-permute-done.refs_0_.refs_1_
  51.9 2.7 %collective-permute-start.4 = (f32[32,8,256]{2,1,0:T(8,128)S(1)}, f32[32,8,256]{2,1,0:T(8,128)S(1)}, u32[]{:S(2)}, u32[]{:S(2)}) collective-permute-start(f32[32,8,256]{2,1,0:T(8,128)S(1)} %collective-permute-done.refs_0_.refs_1_), channel_id=1, source_target_pairs={{0,1},{1,0},{2,3},{3,2},{4,5},{5,4},{6,7},{7,6},{8,9},{9,8},{10,11... | collective-permute-start | bytes 786440 | tf_op jit(solution)/shard_map/ppermute | solution.py:305
  54.6 2.5 %collective-permute-done.1.refs_1_.refs_2_ = f32[32,8,256]{2,1,0:T(8,128)S(1)} collective-permute-done((f32[32,8,256]{2,1,0:T(8,128)S(1)}, f32[32,8,256]{2,1,0:T(8,128)S(1)}, u32[]{:S(2)}, u32[]{:S(2)}) %collective-permute-start.1) | collective-permute-done | bytes 262176 | tf_op jit(solution)/shard_map/ppermute | solution.py:301
  57.0 0.7 collective-permute-start.5
  57.7 0.0 copy-done
  57.7 0.0 collective-permute-done.3.refs_2_.refs_4_
  57.7 0.0 collective-permute-done.6.refs_3_.refs_7_
  57.7 0.8 %gram.1.refs_4_ = f32[256,256]{1,0:T(8,128)S(1)} custom-call(f32[32,8,256]{2,1,0:T(8,128)S(1)} %all-to-all-done.1.refs_0_, f32[32,8,256]{2,1,0:T(8,128)S(1)} %collective-permute-done.2.refs_1_.refs_3_, f32[32,8,256]{2,1,0:T(8,128)S(1)} %collective-permute-done.3.refs_2_.refs_4_, f32[32,8,256]{2,1,0:T(8,128)S(1)} %collective-permute-done.6.refs_3_.refs_7_), custom_call_target="tpu_custom_call" | custom-call | tf_op jit(solution)/shard_map/gram/pallas_call | solution.py:244
  58.5 0.0 collective-permute-done.4.refs_2_.refs_5_
  58.6 0.3 collective-permute-done.5.refs_3_.refs_6_
  58.9 8.6 %factor.1.refs_8_ = f32[256,256]{1,0:T(8,128)S(1)} custom-call(f32[32,8,256]{2,1,0:T(8,128)S(1)} %collective-permute-done.refs_0_.refs_1_, f32[32,8,256]{2,1,0:T(8,128)S(1)} %collective-permute-done.1.refs_1_.refs_2_, f32[32,8,256]{2,1,0:T(8,128)S(1)} %collective-permute-done.4.refs_2_.refs_5_, f32[32,8,256]{2,1,0:T(8,128)S(1)} %collective-permute-done.5.refs_3_.refs_6_, ...), custom_call_target="tpu_custom_call" | custom-call | tf_op jit(solution)/shard_map/factor/pallas_call | solution.py:257
  67.5 0.0 all-to-all-done.2.refs_9_
  67.5 2.7 %core.1 = (f32[64,256]{1,0:T(8,128)}, bf16[128,256]{1,0:T(8,128)(2,1)}) custom-call(f32[32,8,256]{2,1,0:T(8,128)S(1)} %all-to-all-done.1.refs_0_, f32[32,8,256]{2,1,0:T(8,128)S(1)} %collective-permute-done.refs_0_.refs_1_, f32[32,8,256]{2,1,0:T(8,128)S(1)} %collective-permute-done.1.refs_1_.refs_2_, ...), custom_call_target="tpu_custom_call" | custom-call | tf_op jit(solution)/shard_map/core/pallas_call | solution.py:271
  (2 shorter events, 0.0 us)
Async XLA Ops:
  13.8 22.3 %all-to-all-start.1 = ((f32[32,8,256]{2,1,0:T(8,128)}), f32[32,8,256]{2,1,0:T(8,128)S(1)}, u32[]{:S(2)}, u32[]{:S(2)}) async-start(f32[32,8,256]{2,1,0:T(8,128)} %broadcast_in_dim.3), calls=%async_computation.1 | async-start | bytes 524288 | tf_op jit(solution)/shard_map/all_to_all | solution.py:297
  28.7 29.0 %copy-start = (s32[8]{0:T(128)S(1)}, s32[8]{0:T(128)}, u32[]{:S(2)}) copy-start(s32[8]{0:T(128)} %counts_ref.1) | copy-start | bytes 100
  36.2 31.3 %all-to-all-start.2 = ((bf16[32,64,128]{2,1,0:T(8,128)(2,1)}), bf16[32,64,128]{2,1,0:T(8,128)(2,1)S(1)}, u32[]{:S(2)}, u32[]{:S(2)}) async-start(bf16[32,64,128]{2,1,0:T(8,128)(2,1)} %spread.1), calls=%async_computation.2 | async-start | bytes 1048576 | tf_op jit(solution)/shard_map/all_to_all | solution.py:303
  40.9 6.2 %collective-permute-start.2 = (f32[32,8,256]{2,1,0:T(8,128)S(1)}, f32[32,8,256]{2,1,0:T(8,128)S(1)}, u32[]{:S(2)}, u32[]{:S(2)}) collective-permute-start(f32[32,8,256]{2,1,0:T(8,128)S(1)} %all-to-all-done.1.refs_0_), channel_id=1, source_target_pairs={{0,6},{1,7},{2,0},{3,1},{4,2},{5,3},{6,4},{7,5},{8,14},{9,15},{10,... | collective-permute-start | bytes 786440 | tf_op jit(solution)/shard_map/ppermute | solution.py:301
  41.9 10.0 %collective-permute-start = (f32[32,8,256]{2,1,0:T(8,128)S(1)}, f32[32,8,256]{2,1,0:T(8,128)S(1)}, u32[]{:S(2)}, u32[]{:S(2)}) collective-permute-start(f32[32,8,256]{2,1,0:T(8,128)S(1)} %all-to-all-done.1.refs_0_), channel_id=1, source_target_pairs={{0,4},{1,5},{2,6},{3,7},{4,0},{5,1},{6,2},{7,3},{8,12},{9,13},{10,... | collective-permute-start | bytes 786440 | tf_op jit(solution)/shard_map/ppermute | solution.py:301
  43.0 14.0 %collective-permute-start.1 = (f32[32,8,256]{2,1,0:T(8,128)S(1)}, f32[32,8,256]{2,1,0:T(8,128)S(1)}, u32[]{:S(2)}, u32[]{:S(2)}) collective-permute-start(f32[32,8,256]{2,1,0:T(8,128)S(1)} %all-to-all-done.1.refs_0_), channel_id=1, source_target_pairs={{0,2},{1,3},{2,4},{3,5},{4,6},{5,7},{6,0},{7,1},{8,10},{9,11},{10,... | collective-permute-start | bytes 786440 | tf_op jit(solution)/shard_map/ppermute | solution.py:301
  43.1 14.7 %collective-permute-start.3 = (f32[32,8,256]{2,1,0:T(8,128)S(1)}, f32[32,8,256]{2,1,0:T(8,128)S(1)}, u32[]{:S(2)}, u32[]{:S(2)}) collective-permute-start(f32[32,8,256]{2,1,0:T(8,128)S(1)} %all-to-all-done.1.refs_0_), channel_id=1, source_target_pairs={{0,1},{1,0},{2,3},{3,2},{4,5},{5,4},{6,7},{7,6},{8,9},{9,8},{10,11... | collective-permute-start | bytes 786440 | tf_op jit(solution)/shard_map/ppermute | solution.py:305
  47.1 10.6 %collective-permute-start.6 = (f32[32,8,256]{2,1,0:T(8,128)S(1)}, f32[32,8,256]{2,1,0:T(8,128)S(1)}, u32[]{:S(2)}, u32[]{:S(2)}) collective-permute-start(f32[32,8,256]{2,1,0:T(8,128)S(1)} %collective-permute-done.2.refs_1_.refs_3_), channel_id=1, source_target_pairs={{0,1},{1,0},{2,3},{3,2},{4,5},{5,4},{6,7},{7,6},{8,9},{9,8},{10,11... | collective-permute-start | bytes 786440 | tf_op jit(solution)/shard_map/ppermute | solution.py:305
  51.9 6.7 %collective-permute-start.4 = (f32[32,8,256]{2,1,0:T(8,128)S(1)}, f32[32,8,256]{2,1,0:T(8,128)S(1)}, u32[]{:S(2)}, u32[]{:S(2)}) collective-permute-start(f32[32,8,256]{2,1,0:T(8,128)S(1)} %collective-permute-done.refs_0_.refs_1_), channel_id=1, source_target_pairs={{0,1},{1,0},{2,3},{3,2},{4,5},{5,4},{6,7},{7,6},{8,9},{9,8},{10,11... | collective-permute-start | bytes 786440 | tf_op jit(solution)/shard_map/ppermute | solution.py:305
  57.0 1.8 %collective-permute-start.5 = (f32[32,8,256]{2,1,0:T(8,128)S(1)}, f32[32,8,256]{2,1,0:T(8,128)S(1)}, u32[]{:S(2)}, u32[]{:S(2)}) collective-permute-start(f32[32,8,256]{2,1,0:T(8,128)S(1)} %collective-permute-done.1.refs_1_.refs_2_), channel_id=1, source_target_pairs={{0,1},{1,0},{2,3},{3,2},{4,5},{5,4},{6,7},{7,6},{8,9},{9,8},{10,11... | collective-permute-start | bytes 786440 | tf_op jit(solution)/shard_map/ppermute | solution.py:305
where the time goes:
time: 70.6 us; the launch traced here: 70.2 us
  starting transfers between devices  28.3 us (40%)
  Pallas kernels  17.8 us (25%)
  waiting for transfers between devices  12 us (17%)
  blocking collectives  10.6 us (15%)
  local copies, waits for them, and re-layouts  0.71 us (1%)
  between operations  0.71 us (1%)
    all_to_all x1, starting transfers between devices, local(): column = lax.all_to_all(part, 'gx', 0, 0, tiled=True)  11 us
    all_to_all x1, blocking collectives, local(): lax.all_to_all(total.reshape(members, -1, sketch), 'yz', 0, 0, tiled=True)  10.6 us
    ppermute x4, starting transfers between devices, local(): pieces = pieces + [lax.ppermute(piece, 'yz', swap) for piece in pieces]  10.4 us
    pallas_call x1, Pallas kernels, inverse_factor(): pl.pallas_call(factor_kernel, out_shape=pltpu.VMEM((size, size), F32), in...  8.58 us
    all_to_all x1, waiting for transfers between devices, local(): column = lax.all_to_all(part, 'gx', 0, 0, tiled=True)  7.47 us
    all_to_all x1, starting transfers between devices, local(): moved = lax.all_to_all(chunks, 'gx', 0, 0, tiled=True)  4.74 us
    ppermute x3, waiting for transfers between devices, local(): pieces.append(lax.ppermute(column, 'yz', turn))  4.24 us
    pallas_call x1, Pallas kernels, spread_columns(): pl.pallas_call(spread_kernel, out_shape=jax.ShapeDtypeStruct((chunks * SH...  3.8 us
  transfers between devices with their start and end apart: 9, of which 4 were waited for; matrix products, arithmetic and copies ran while one was open for 0% of the time, Pallas kernels for 19%

commit v1 on v0

--- a/solution.py
+++ b/solution.py
@@ -14,7 +14,6 @@
 STEPS = (0, 2, 1, 3)
 EARLY = (0, 3)
 SLOTS = 4
-SHARES = 4
 ROOM = pltpu.CompilerParams(vmem_limit_bytes=24 << 20)
 
 
@@ -96,15 +95,14 @@
 
 def spread_columns(tensor):
     rows, slots, width = tensor.shape
-    share = width // SHARES
-    chunks = share * slots // 128
+    vmem = pl.BlockSpec(memory_space=pltpu.VMEM)
     return pl.pallas_call(
         spread_kernel,
-        out_shape=jax.ShapeDtypeStruct((chunks * SHARES, rows, 128), BF16),
-        grid=(SHARES,),
-        in_specs=[pl.BlockSpec((rows, slots, share), lambda number: (0, 0, number))],
-        out_specs=pl.BlockSpec((chunks, rows, 128), lambda number: (number, 0, 0)),
+        out_shape=jax.ShapeDtypeStruct((width * slots // 128, rows, 128), BF16),
+        in_specs=[vmem],
+        out_specs=vmem,
         name="spread",
+        compiler_params=ROOM,
     )(tensor)
 
 

time: 70.6 us -> 70.7 us (level)
  Pallas kernels: 17.8 us -> 15.4 us
  waiting for transfers between devices: 12 us -> 14.4 us
    pallas_call x1, Pallas kernels: 3.8 us -> 1.45 us  [spread_columns(): pl.pallas_call(spread_kernel, out_shape=jax.ShapeDtypeStruct((width * slo...]
    all_to_all x1, waiting for transfers between devices: 7.47 us -> 9.8 us  [local(): column = lax.all_to_all(part, 'gx', 0, 0, tiled=True)]
  transfers between devices with their start and end apart: 9 -> 9, of which waited for: 4 -> 4; matrix products, arithmetic and copies ran while one was open for 0% -> 0% of each run, Pallas kernels for 19% -> 15%
where the time goes in v1:
time: 70.7 us; the launch traced here: 70.4 us
  starting transfers between devices  28.3 us (40%)
  Pallas kernels  15.4 us (22%)
  waiting for transfers between devices  14.4 us (20%)
  blocking collectives  10.7 us (15%)
  local copies, waits for them, and re-layouts  0.73 us (1%)
  between operations  0.73 us (1%)
    all_to_all x1, starting transfers between devices, local(): column = lax.all_to_all(part, 'gx', 0, 0, tiled=True)  11 us
    all_to_all x1, blocking collectives, local(): lax.all_to_all(total.reshape(members, -1, sketch), 'yz', 0, 0, tiled=True)  10.7 us
    ppermute x4, starting transfers between devices, local(): pieces = pieces + [lax.ppermute(piece, 'yz', swap) for piece in pieces]  10.4 us
    all_to_all x1, waiting for transfers between devices, local(): column = lax.all_to_all(part, 'gx', 0, 0, tiled=True)  9.8 us
    pallas_call x1, Pallas kernels, inverse_factor(): pl.pallas_call(factor_kernel, out_shape=pltpu.VMEM((size, size), F32), in...  8.58 us
    all_to_all x1, starting transfers between devices, local(): moved = lax.all_to_all(chunks, 'gx', 0, 0, tiled=True)  4.74 us
    ppermute x3, waiting for transfers between devices, local(): pieces.append(lax.ppermute(column, 'yz', turn))  4.24 us
    pallas_call x1, Pallas kernels, core_and_basis(): pl.pallas_call(core_kernel, out_shape=(jax.ShapeDtypeStruct((parts * line...  2.73 us
  transfers between devices with their start and end apart: 9, of which 4 were waited for; matrix products, arithmetic and copies ran while one was open for 0% of the time, Pallas kernels for 15%

profile of v1, /device:TPU:1, one launch (start us, length us, event | category | flops | bytes accessed | tf_op | source)
XLA Modules:
  0.0 70.4 jit_solution(6044012601303636961)
XLA Ops:
  0.6 1.9 %sketch.1 = f32[64,256]{1,0:T(8,128)S(1)} custom-call(bf16[64,4,1024]{2,1,0:T(4,128)(2,1)} %tensor_ref.3, s32[8]{0:T(128)} %counts_ref.1, f32[16,1024]{1,0:T(8,128)} %scale_ref.1, s32[16,256]{1,0:T(8,128)} %samples_ref.1), custom_call_target="tpu_custom_call" | custom-call | tf_op jit(solution)/shard_map/sketch/pallas_call | solution.py:86
  2.5 0.0 copy-start
  2.5 10.7 %all_to_all.15 = f32[8,8,256]{2,1,0:T(8,128)S(1)} all-to-all(f32[8,8,256]{2,1,0:T(8,128)S(1)} %bitcast.4), channel_id=1, replica_groups=mesh['gx'=32,'yz'=8] {'yz'}, dimensions={0} | all-to-all | bytes 131072 | tf_op jit(solution)/shard_map/all_to_all | solution.py:293
  13.3 0.7 %broadcast_in_dim.3 = f32[32,8,256]{2,1,0:T(8,128)} broadcast(f32[8,256]{1,0:T(8,128)S(1)} %reduce_sum.9), dimensions={1,2} | broadcast | bytes 270336 | tf_op jit(solution)/shard_map/broadcast_in_dim | solution.py:294
  14.0 11.0 %all-to-all-start.1 = ((f32[32,8,256]{2,1,0:T(8,128)}), f32[32,8,256]{2,1,0:T(8,128)S(1)}, u32[]{:S(2)}, u32[]{:S(2)}) async-start(f32[32,8,256]{2,1,0:T(8,128)} %broadcast_in_dim.3), calls=%async_computation.1 | async-start | bytes 524288 | tf_op jit(solution)/shard_map/all_to_all | solution.py:295
  25.0 0.0 copy-done
  25.0 1.5 %spread.1 = bf16[32,64,128]{2,1,0:T(8,128)(2,1)} custom-call(bf16[64,4,1024]{2,1,0:T(4,128)(2,1)S(1)} %copy-done), custom_call_target="tpu_custom_call" | custom-call | tf_op jit(solution)/shard_map/spread/pallas_call | solution.py:99
  26.5 0.0 copy-start.1
  26.5 9.8 %all-to-all-done.1.refs_0_ = f32[32,8,256]{2,1,0:T(8,128)S(1)} async-done(((f32[32,8,256]{2,1,0:T(8,128)}), f32[32,8,256]{2,1,0:T(8,128)S(1)}, u32[]{:S(2)}, u32[]{:S(2)}) %all-to-all-start.1) | async-done | bytes 262176 | tf_op jit(solution)/shard_map/all_to_all | solution.py:295
  36.3 4.7 %all-to-all-start.2 = ((bf16[32,64,128]{2,1,0:T(8,128)(2,1)}), bf16[32,64,128]{2,1,0:T(8,128)(2,1)S(1)}, u32[]{:S(2)}, u32[]{:S(2)}) async-start(bf16[32,64,128]{2,1,0:T(8,128)(2,1)} %spread.1), calls=%async_computation.2 | async-start | bytes 1048576 | tf_op jit(solution)/shard_map/all_to_all | solution.py:301
  41.1 1.0 %collective-permute-start.2 = (f32[32,8,256]{2,1,0:T(8,128)S(1)}, f32[32,8,256]{2,1,0:T(8,128)S(1)}, u32[]{:S(2)}, u32[]{:S(2)}) collective-permute-start(f32[32,8,256]{2,1,0:T(8,128)S(1)} %all-to-all-done.1.refs_0_), channel_id=1, source_target_pairs={{0,6},{1,7},{2,0},{3,1},{4,2},{5,3},{6,4},{7,5},{8,14},{9,15},{10,... | collective-permute-start | bytes 786440 | tf_op jit(solution)/shard_map/ppermute | solution.py:299
  42.0 1.2 %collective-permute-start = (f32[32,8,256]{2,1,0:T(8,128)S(1)}, f32[32,8,256]{2,1,0:T(8,128)S(1)}, u32[]{:S(2)}, u32[]{:S(2)}) collective-permute-start(f32[32,8,256]{2,1,0:T(8,128)S(1)} %all-to-all-done.1.refs_0_), channel_id=1, source_target_pairs={{0,4},{1,5},{2,6},{3,7},{4,0},{5,1},{6,2},{7,3},{8,12},{9,13},{10,... | collective-permute-start | bytes 786440 | tf_op jit(solution)/shard_map/ppermute | solution.py:299
  43.2 0.0 collective-permute-start.1
  43.2 2.3 %collective-permute-start.3 = (f32[32,8,256]{2,1,0:T(8,128)S(1)}, f32[32,8,256]{2,1,0:T(8,128)S(1)}, u32[]{:S(2)}, u32[]{:S(2)}) collective-permute-start(f32[32,8,256]{2,1,0:T(8,128)S(1)} %all-to-all-done.1.refs_0_), channel_id=1, source_target_pairs={{0,1},{1,0},{2,3},{3,2},{4,5},{5,4},{6,7},{7,6},{8,9},{9,8},{10,11... | collective-permute-start | bytes 786440 | tf_op jit(solution)/shard_map/ppermute | solution.py:303
  45.5 1.8 %collective-permute-done.2.refs_1_.refs_3_ = f32[32,8,256]{2,1,0:T(8,128)S(1)} collective-permute-done((f32[32,8,256]{2,1,0:T(8,128)S(1)}, f32[32,8,256]{2,1,0:T(8,128)S(1)}, u32[]{:S(2)}, u32[]{:S(2)}) %collective-permute-start.2) | collective-permute-done | bytes 262176 | tf_op jit(solution)/shard_map/ppermute | solution.py:299
  47.3 4.8 %collective-permute-start.6 = (f32[32,8,256]{2,1,0:T(8,128)S(1)}, f32[32,8,256]{2,1,0:T(8,128)S(1)}, u32[]{:S(2)}, u32[]{:S(2)}) collective-permute-start(f32[32,8,256]{2,1,0:T(8,128)S(1)} %collective-permute-done.2.refs_1_.refs_3_), channel_id=1, source_target_pairs={{0,1},{1,0},{2,3},{3,2},{4,5},{5,4},{6,7},{7,6},{8,9},{9,8},{10,11... | collective-permute-start | bytes 786440 | tf_op jit(solution)/shard_map/ppermute | solution.py:303
  52.0 0.0 collective-permute-done.refs_0_.refs_1_
  52.0 2.7 %collective-permute-start.4 = (f32[32,8,256]{2,1,0:T(8,128)S(1)}, f32[32,8,256]{2,1,0:T(8,128)S(1)}, u32[]{:S(2)}, u32[]{:S(2)}) collective-permute-start(f32[32,8,256]{2,1,0:T(8,128)S(1)} %collective-permute-done.refs_0_.refs_1_), channel_id=1, source_target_pairs={{0,1},{1,0},{2,3},{3,2},{4,5},{5,4},{6,7},{7,6},{8,9},{9,8},{10,11... | collective-permute-start | bytes 786440 | tf_op jit(solution)/shard_map/ppermute | solution.py:303
  54.7 2.5 %collective-permute-done.1.refs_1_.refs_2_ = f32[32,8,256]{2,1,0:T(8,128)S(1)} collective-permute-done((f32[32,8,256]{2,1,0:T(8,128)S(1)}, f32[32,8,256]{2,1,0:T(8,128)S(1)}, u32[]{:S(2)}, u32[]{:S(2)}) %collective-permute-start.1) | collective-permute-done | bytes 262176 | tf_op jit(solution)/shard_map/ppermute | solution.py:299
  57.2 0.7 collective-permute-start.5
  57.9 0.0 copy-done.1
  57.9 0.0 collective-permute-done.3.refs_2_.refs_4_
  57.9 0.0 collective-permute-done.6.refs_3_.refs_7_
  57.9 0.8 %gram.1.refs_4_ = f32[256,256]{1,0:T(8,128)S(1)} custom-call(f32[32,8,256]{2,1,0:T(8,128)S(1)} %all-to-all-done.1.refs_0_, f32[32,8,256]{2,1,0:T(8,128)S(1)} %collective-permute-done.2.refs_1_.refs_3_, f32[32,8,256]{2,1,0:T(8,128)S(1)} %collective-permute-done.3.refs_2_.refs_4_, f32[32,8,256]{2,1,0:T(8,128)S(1)} %collective-permute-done.6.refs_3_.refs_7_), custom_call_target="tpu_custom_call" | custom-call | tf_op jit(solution)/shard_map/gram/pallas_call | solution.py:242
  58.7 0.0 collective-permute-done.4.refs_2_.refs_5_
  58.7 0.3 collective-permute-done.5.refs_3_.refs_6_
  59.0 8.6 %factor.1.refs_8_ = f32[256,256]{1,0:T(8,128)S(1)} custom-call(f32[32,8,256]{2,1,0:T(8,128)S(1)} %collective-permute-done.refs_0_.refs_1_, f32[32,8,256]{2,1,0:T(8,128)S(1)} %collective-permute-done.1.refs_1_.refs_2_, f32[32,8,256]{2,1,0:T(8,128)S(1)} %collective-permute-done.4.refs_2_.refs_5_, f32[32,8,256]{2,1,0:T(8,128)S(1)} %collective-permute-done.5.refs_3_.refs_6_, ...), custom_call_target="tpu_custom_call" | custom-call | tf_op jit(solution)/shard_map/factor/pallas_call | solution.py:255
  67.6 0.0 all-to-all-done.2.refs_9_
  67.6 2.7 %core.1 = (f32[64,256]{1,0:T(8,128)}, bf16[128,256]{1,0:T(8,128)(2,1)}) custom-call(f32[32,8,256]{2,1,0:T(8,128)S(1)} %all-to-all-done.1.refs_0_, f32[32,8,256]{2,1,0:T(8,128)S(1)} %collective-permute-done.refs_0_.refs_1_, f32[32,8,256]{2,1,0:T(8,128)S(1)} %collective-permute-done.1.refs_1_.refs_2_, ...), custom_call_target="tpu_custom_call" | custom-call | tf_op jit(solution)/shard_map/core/pallas_call | solution.py:269
  (2 shorter events, 0.0 us)
Async XLA Ops:
  2.5 22.5 %copy-start = (bf16[64,4,1024]{2,1,0:T(4,128)(2,1)S(1)}, bf16[64,4,1024]{2,1,0:T(4,128)(2,1)}, u32[]{:S(2)}) copy-start(bf16[64,4,1024]{2,1,0:T(4,128)(2,1)} %tensor_ref.3) | copy-start | bytes 1572868
  14.0 22.3 %all-to-all-start.1 = ((f32[32,8,256]{2,1,0:T(8,128)}), f32[32,8,256]{2,1,0:T(8,128)S(1)}, u32[]{:S(2)}, u32[]{:S(2)}) async-start(f32[32,8,256]{2,1,0:T(8,128)} %broadcast_in_dim.3), calls=%async_computation.1 | async-start | bytes 524288 | tf_op jit(solution)/shard_map/all_to_all | solution.py:295
  26.5 31.4 %copy-start.1 = (s32[8]{0:T(128)S(1)}, s32[8]{0:T(128)}, u32[]{:S(2)}) copy-start(s32[8]{0:T(128)} %counts_ref.1) | copy-start | bytes 100
  36.3 31.3 %all-to-all-start.2 = ((bf16[32,64,128]{2,1,0:T(8,128)(2,1)}), bf16[32,64,128]{2,1,0:T(8,128)(2,1)S(1)}, u32[]{:S(2)}, u32[]{:S(2)}) async-start(bf16[32,64,128]{2,1,0:T(8,128)(2,1)} %spread.1), calls=%async_computation.2 | async-start | bytes 1048576 | tf_op jit(solution)/shard_map/all_to_all | solution.py:301
  41.1 6.2 %collective-permute-start.2 = (f32[32,8,256]{2,1,0:T(8,128)S(1)}, f32[32,8,256]{2,1,0:T(8,128)S(1)}, u32[]{:S(2)}, u32[]{:S(2)}) collective-permute-start(f32[32,8,256]{2,1,0:T(8,128)S(1)} %all-to-all-done.1.refs_0_), channel_id=1, source_target_pairs={{0,6},{1,7},{2,0},{3,1},{4,2},{5,3},{6,4},{7,5},{8,14},{9,15},{10,... | collective-permute-start | bytes 786440 | tf_op jit(solution)/shard_map/ppermute | solution.py:299
  42.0 10.0 %collective-permute-start = (f32[32,8,256]{2,1,0:T(8,128)S(1)}, f32[32,8,256]{2,1,0:T(8,128)S(1)}, u32[]{:S(2)}, u32[]{:S(2)}) collective-permute-start(f32[32,8,256]{2,1,0:T(8,128)S(1)} %all-to-all-done.1.refs_0_), channel_id=1, source_target_pairs={{0,4},{1,5},{2,6},{3,7},{4,0},{5,1},{6,2},{7,3},{8,12},{9,13},{10,... | collective-permute-start | bytes 786440 | tf_op jit(solution)/shard_map/ppermute | solution.py:299
  43.2 14.0 %collective-permute-start.1 = (f32[32,8,256]{2,1,0:T(8,128)S(1)}, f32[32,8,256]{2,1,0:T(8,128)S(1)}, u32[]{:S(2)}, u32[]{:S(2)}) collective-permute-start(f32[32,8,256]{2,1,0:T(8,128)S(1)} %all-to-all-done.1.refs_0_), channel_id=1, source_target_pairs={{0,2},{1,3},{2,4},{3,5},{4,6},{5,7},{6,0},{7,1},{8,10},{9,11},{10,... | collective-permute-start | bytes 786440 | tf_op jit(solution)/shard_map/ppermute | solution.py:299
  43.2 14.7 %collective-permute-start.3 = (f32[32,8,256]{2,1,0:T(8,128)S(1)}, f32[32,8,256]{2,1,0:T(8,128)S(1)}, u32[]{:S(2)}, u32[]{:S(2)}) collective-permute-start(f32[32,8,256]{2,1,0:T(8,128)S(1)} %all-to-all-done.1.refs_0_), channel_id=1, source_target_pairs={{0,1},{1,0},{2,3},{3,2},{4,5},{5,4},{6,7},{7,6},{8,9},{9,8},{10,11... | collective-permute-start | bytes 786440 | tf_op jit(solution)/shard_map/ppermute | solution.py:303
  47.3 10.6 %collective-permute-start.6 = (f32[32,8,256]{2,1,0:T(8,128)S(1)}, f32[32,8,256]{2,1,0:T(8,128)S(1)}, u32[]{:S(2)}, u32[]{:S(2)}) collective-permute-start(f32[32,8,256]{2,1,0:T(8,128)S(1)} %collective-permute-done.2.refs_1_.refs_3_), channel_id=1, source_target_pairs={{0,1},{1,0},{2,3},{3,2},{4,5},{5,4},{6,7},{7,6},{8,9},{9,8},{10,11... | collective-permute-start | bytes 786440 | tf_op jit(solution)/shard_map/ppermute | solution.py:303
  52.0 6.7 %collective-permute-start.4 = (f32[32,8,256]{2,1,0:T(8,128)S(1)}, f32[32,8,256]{2,1,0:T(8,128)S(1)}, u32[]{:S(2)}, u32[]{:S(2)}) collective-permute-start(f32[32,8,256]{2,1,0:T(8,128)S(1)} %collective-permute-done.refs_0_.refs_1_), channel_id=1, source_target_pairs={{0,1},{1,0},{2,3},{3,2},{4,5},{5,4},{6,7},{7,6},{8,9},{9,8},{10,11... | collective-permute-start | bytes 786440 | tf_op jit(solution)/shard_map/ppermute | solution.py:303
  57.2 1.8 %collective-permute-start.5 = (f32[32,8,256]{2,1,0:T(8,128)S(1)}, f32[32,8,256]{2,1,0:T(8,128)S(1)}, u32[]{:S(2)}, u32[]{:S(2)}) collective-permute-start(f32[32,8,256]{2,1,0:T(8,128)S(1)} %collective-permute-done.1.refs_1_.refs_2_), channel_id=1, source_target_pairs={{0,1},{1,0},{2,3},{3,2},{4,5},{5,4},{6,7},{7,6},{8,9},{9,8},{10,11... | collective-permute-start | bytes 786440 | tf_op jit(solution)/shard_map/ppermute | solution.py:303
